TPU v7x, 32 devices: a whole 2x2x4 slice. The times are simulated.
32 devices in a mesh: dp: 16 (over z, y, core), tensor: 2 (over x).
Axes of the slice: x: 2, y: 2, z: 4, core: 2. Of those that a mesh axis runs over, the one named last changes fastest.
Arguments:
- residual_in: float32 [8192, 1024], P(('dp', 'tensor')), may hold values from -6 to 6
- out_cotangent: float32 [8192, 1024], P(('dp', 'tensor')), may hold values from -6 to 6
- seq_lengths: int32 [4], replicated, may hold values from 1 to 4096, 8192 in all
- qkv_weight: float32 [1024, 3072], P('dp', 'tensor'), may hold values from -1 to 1
- out_weight: float32 [1024, 1024], P('tensor', 'dp'), may hold values from -2 to 2
- in_weight: float32 [1024, 2, 2624], P('dp', None, 'tensor'), may hold values from -0.1875 to 0.1875
- down_weight: float32 [2624, 1024], P('tensor', 'dp'), may hold values from -0.125 to 0.125
- norm_gains: float32 [2, 1024], replicated, may hold values from 0.5 to 1.5
- qkv_moments: float32 [2, 1024, 3072], P(None, 'dp', 'tensor'), may hold values from -8192 to 8192, as said below
- out_moments: float32 [2, 1024, 1024], P(None, 'tensor', 'dp'), may hold values from -8192 to 8192, as said below
- in_moments: float32 [2, 1024, 2, 2624], P(None, 'dp', None, 'tensor'), may hold values from -8192 to 8192, as said below
- down_moments: float32 [2, 2624, 1024], P(None, 'tensor', 'dp'), may hold values from -8192 to 8192, as said below
- gain_moments: float32 [2, 2, 1024], replicated, may hold values from -8192 to 8192, as said below
Outputs:
- block_out: float32 [8192, 1024], P(('dp', 'tensor'))
- residual_grad: float32 [8192, 1024], P(('dp', 'tensor'))
- qkv_grad: float32 [1024, 3072], P('dp', 'tensor')
- out_weight_grad: float32 [1024, 1024], P('tensor', 'dp')
- in_grad: float32 [1024, 2, 2624], P('dp', None, 'tensor')
- down_grad: float32 [2624, 1024], P('tensor', 'dp')
- gains_grad: float32 [2, 1024], replicated
- new_qkv: float32 [1024, 3072], P('dp', 'tensor')
- new_out: float32 [1024, 1024], P('tensor', 'dp')
- new_in: float32 [1024, 2, 2624], P('dp', None, 'tensor')
- new_down: float32 [2624, 1024], P('tensor', 'dp')
- new_gains: float32 [2, 1024], replicated
- new_qkv_moments: float32 [2, 1024, 3072], P(None, 'dp', 'tensor')
- new_out_moments: float32 [2, 1024, 1024], P(None, 'tensor', 'dp')
- new_in_moments: float32 [2, 1024, 2, 2624], P(None, 'dp', None, 'tensor')
- new_down_moments: float32 [2, 2624, 1024], P(None, 'tensor', 'dp')
- new_gain_moments: float32 [2, 2, 1024], replicated
Inputs may be any that keep to these rules, and one draw needn't show every extreme that they name: `seq_lengths`: the lengths sum to 8192; the longest is exactly 4096. `qkv_moments`: index 0 is the first moment, index 1 the second moment, which is positive. `out_moments`: index 0 is the first moment, index 1 the second moment, which is positive. `in_moments`: index 0 is the first moment, index 1 the second moment, which is positive. `down_moments`: index 0 is the first moment, index 1 the second moment, which is positive. `gain_moments`: index 0 is the first moment, index 1 the second moment, which is positive.
All inputs are finite; a program needn't handle non-finite values.
Results may differ from a plain program's by a relative error of at most 0.019.
Values may be sent and summed in bfloat16 or wider, within the bound.
A program may use at most 128 MiB of HBM per device.

v0:
```python
import math

import jax
import jax.numpy as jnp
from jax import lax
from jax.sharding import PartitionSpec as P

HD = 64
HALF_WIN = 64
STEP = 3


NORM_EPS = 1e-05
ROPE_BASE = 10000.0
BETA_ONE = 0.9
BETA_TWO = 0.999
ADAM_EPS = 1e-08
LEARN_RATE = 0.005
DECAY_RATE = 0.1
MASKED = -1e30


def padded(value, sides, width):
    for axis, dim in sides:
        size, length = (lax.axis_size(axis), value.shape[dim])
        up = [(i, (i + 1) % size) for i in range(size - 1)]
        down = [(j, i) for i, j in up]
        last = lax.slice_in_dim(value, length - width, length, axis=dim)
        first = lax.slice_in_dim(value, 0, width, axis=dim)
        before = lax.ppermute(last, axis, up)
        after = lax.ppermute(first, axis, down)
        value = jnp.concatenate([before, value, after], axis=dim)
    return value


def norm_forward(rows, gain):
    row_mean = jnp.mean(rows, axis=-1, keepdims=True)
    centered = rows - row_mean
    inv_std = lax.rsqrt(jnp.mean(centered * centered, axis=-1, keepdims=True) + NORM_EPS)
    normed = centered * inv_std
    return (normed, inv_std, normed * gain)


def norm_backward(grad_out, normed, inv_std, gain):
    scaled = grad_out * gain
    grad_rows = inv_std * (
        scaled
        - jnp.mean(scaled, axis=-1, keepdims=True)
        - normed * jnp.mean(scaled * normed, axis=-1, keepdims=True)
    )
    return (grad_rows, jnp.sum(grad_out * normed, axis=0))


def seq_coords(seq_lengths, places):
    seq_ends = jnp.cumsum(seq_lengths, dtype=jnp.int32)
    passed = (seq_ends[None, :] <= places[:, None]).astype(jnp.int32)
    seq_ids = jnp.sum(passed, axis=1, dtype=jnp.int32)
    seq_start = jnp.sum(passed * seq_lengths[None, :], axis=1, dtype=jnp.int32)
    return (seq_ids, places - seq_start)


def rotary_tables(offsets, head_dim):
    half_dim = head_dim // 2
    inv_freq = ROPE_BASE ** (-2.0 * jnp.arange(half_dim).astype(jnp.float32) / head_dim)
    angles = offsets.astype(jnp.float32)[:, None] * inv_freq[None, :]
    cos_table = jnp.cos(angles)
    sin_table = jnp.sin(angles)
    return (
        jnp.concatenate([cos_table, cos_table], axis=-1),
        jnp.concatenate([sin_table, sin_table], axis=-1),
    )


def rotate(feats, cos_table, sin_table):
    half_dim = feats.shape[-1] // 2
    turned = jnp.concatenate([-feats[..., half_dim:], feats[..., :half_dim]], axis=-1)
    return feats * cos_table[:, None, :] + turned * sin_table[:, None, :]


def unrotate(grads, cos_table, sin_table):
    half_dim = grads.shape[-1] // 2
    spun = grads * sin_table[:, None, :]
    back = jnp.concatenate([spun[..., half_dim:], -spun[..., :half_dim]], axis=-1)
    return grads * cos_table[:, None, :] + back


def gelu_parts(pre_act):
    normal_cdf = 0.5 * (1.0 + lax.erf(pre_act * (1.0 / math.sqrt(2.0))))
    density = jnp.exp(-0.5 * pre_act * pre_act) * (1.0 / math.sqrt(2.0 * math.pi))
    return (pre_act * normal_cdf, normal_cdf + pre_act * density)


def block_mask(query_ids, key_ids, reach):
    query_count = query_ids.shape[0]
    key_count = key_ids.shape[0]
    distance = (
        jnp.arange(key_count, dtype=jnp.int32)[None, :]
        - reach
        - jnp.arange(query_count, dtype=jnp.int32)[:, None]
    )
    return (query_ids[:, None] == key_ids[None, :]) & (jnp.abs(distance) <= reach)


def block_scores(query_rows, key_rows, allowed):
    score_scale = 1.0 / math.sqrt(query_rows.shape[-1])
    scores = (
        jnp.einsum("qhe,khe->hqk", query_rows, key_rows, preferred_element_type=jnp.float32)
        * score_scale
    )
    return jnp.where(allowed[None, :, :], scores, MASKED)


def block_forward(query_rows, key_rows, value_rows, allowed):
    scores = block_scores(query_rows, key_rows, allowed)
    row_max = jnp.max(scores, axis=-1, keepdims=True)
    log_norm = row_max + jnp.log(jnp.sum(jnp.exp(scores - row_max), axis=-1, keepdims=True))
    attn_probs = jnp.exp(scores - log_norm).astype(jnp.bfloat16)
    mixed = jnp.einsum("hqk,khe->qhe", attn_probs, value_rows, preferred_element_type=jnp.float32)
    return (mixed.astype(jnp.bfloat16), log_norm[..., 0])


def block_backward(query_rows, key_rows, value_rows, allowed, log_norm, grad_rows, deltas):
    score_scale = 1.0 / math.sqrt(query_rows.shape[-1])
    scores = block_scores(query_rows, key_rows, allowed)
    probs_full = jnp.exp(scores - log_norm[..., None])
    grad_probs = jnp.einsum(
        "qhe,khe->hqk", grad_rows, value_rows, preferred_element_type=jnp.float32
    )
    grad_scores = (probs_full * (grad_probs - jnp.transpose(deltas)[:, :, None])).astype(
        jnp.bfloat16
    )
    attn_probs = probs_full.astype(jnp.bfloat16)
    grad_queries = (
        jnp.einsum("hqk,khe->qhe", grad_scores, key_rows, preferred_element_type=jnp.float32)
        * score_scale
    )
    grad_keys = (
        jnp.einsum("hqk,qhe->khe", grad_scores, query_rows, preferred_element_type=jnp.float32)
        * score_scale
    )
    grad_values = jnp.einsum(
        "hqk,qhe->khe", attn_probs, grad_rows, preferred_element_type=jnp.float32
    )
    return (grad_queries, grad_keys, grad_values)


def product_rows(matrix, weight, contract_dim):
    return lax.dot_general(
        matrix, weight, (((1,), (contract_dim,)), ((), ())), preferred_element_type=jnp.float32
    )


def across_rows(left, right):
    return lax.dot_general(
        left, right, (((0,), (0,)), ((), ())), preferred_element_type=jnp.float32
    )


def against_cols(left, right):
    return lax.dot_general(
        left, right, (((1,), (1,)), ((), ())), preferred_element_type=jnp.float32
    )


def adam_update(weight, moments, grad, decay):
    first_moment = BETA_ONE * moments[0] + (1.0 - BETA_ONE) * grad
    second_moment = BETA_TWO * moments[1] + (1.0 - BETA_TWO) * grad * grad
    first_hat = first_moment / (1.0 - BETA_ONE**STEP)
    second_hat = second_moment / (1.0 - BETA_TWO**STEP)
    new_weight = weight - LEARN_RATE * (
        first_hat / (jnp.sqrt(second_hat) + ADAM_EPS) + decay * weight
    )
    return (new_weight, jnp.stack([first_moment, second_moment]))


def local(
    residual_in,
    out_cotangent,
    seq_lengths,
    qkv_weight,
    out_weight,
    in_weight,
    down_weight,
    norm_gains,
    qkv_moments,
    out_moments,
    in_moments,
    down_moments,
    gain_moments,
):
    tensor_count = lax.axis_size("tensor")
    data_count = lax.axis_size("dp")
    local_rows = residual_in.shape[0]
    seq_rows = local_rows * tensor_count
    reach = HALF_WIN
    block_rows = min(512, seq_rows)
    span = block_rows + 2 * reach
    qkv_full, out_full, in_full, down_full = (
        lax.all_gather(qkv_weight.astype(jnp.bfloat16), "dp", axis=0, tiled=True),
        lax.all_gather(out_weight.astype(jnp.bfloat16), "dp", axis=1, tiled=True),
        lax.all_gather(in_weight.astype(jnp.bfloat16), "dp", axis=0, tiled=True),
        lax.all_gather(down_weight.astype(jnp.bfloat16), "dp", axis=1, tiled=True),
    )
    model_dim = qkv_full.shape[0]
    head_dim = HD
    local_heads = qkv_full.shape[1] // (3 * head_dim)
    local_hidden = in_full.shape[2]
    head_feats = local_heads * head_dim
    in_flat = in_full.reshape(model_dim, 2 * local_hidden)
    first_token = lax.axis_index("dp") * seq_rows
    places = first_token + jnp.arange(seq_rows, dtype=jnp.int32)
    query_ids, offsets = seq_coords(seq_lengths, places)
    cos_table, sin_table = rotary_tables(offsets, head_dim)
    key_places = first_token - reach + jnp.arange(seq_rows + 2 * reach, dtype=jnp.int32)
    inside = (key_places >= 0) & (key_places < seq_rows * data_count)
    key_ids = jnp.where(inside, seq_coords(seq_lengths, key_places)[0], -1)
    first_normed, first_inv, first_scaled = norm_forward(residual_in, norm_gains[0])
    normed_in = lax.all_gather(first_scaled.astype(jnp.bfloat16), "tensor", axis=0, tiled=True)
    proj = jnp.dot(normed_in, qkv_full, preferred_element_type=jnp.float32).reshape(
        seq_rows, local_heads, 3, head_dim
    )
    queries = rotate(proj[:, :, 0], cos_table, sin_table).astype(jnp.bfloat16)
    keys = rotate(proj[:, :, 1], cos_table, sin_table).astype(jnp.bfloat16)
    values = proj[:, :, 2].astype(jnp.bfloat16)
    key_vals = jnp.concatenate(
        [keys.reshape(seq_rows, head_feats), values.reshape(seq_rows, head_feats)], axis=1
    )
    key_vals_pad = padded(key_vals, (("dp", 0),), reach)
    keys_pad = key_vals_pad[:, :head_feats].reshape(seq_rows + 2 * reach, local_heads, head_dim)
    values_pad = key_vals_pad[:, head_feats:].reshape(seq_rows + 2 * reach, local_heads, head_dim)
    allowed = block_mask(query_ids, key_ids, reach)
    mixed_part, norm_part = block_forward(queries, keys_pad, values_pad, allowed)
    mixed_flat = mixed_part.reshape(seq_rows, head_feats)
    attn_out = lax.psum_scatter(
        product_rows(mixed_flat, out_full, 0), "tensor", scatter_dimension=0, tiled=True
    )
    middle = residual_in + attn_out
    second_normed, second_inv, second_scaled = norm_forward(middle, norm_gains[1])
    ffn_in = lax.all_gather(second_scaled.astype(jnp.bfloat16), "tensor", axis=0, tiled=True)
    both = jnp.dot(ffn_in, in_flat, preferred_element_type=jnp.float32).reshape(
        seq_rows, 2, local_hidden
    )
    activated, slope = gelu_parts(both[:, 0])
    gated = (activated * both[:, 1]).astype(jnp.bfloat16)
    ffn_out = lax.psum_scatter(
        product_rows(gated, down_full, 0).astype(jnp.bfloat16),
        "tensor",
        scatter_dimension=0,
        tiled=True,
    ).astype(jnp.float32)
    block_out = middle + ffn_out
    grad_out_all = lax.all_gather(out_cotangent.astype(jnp.bfloat16), "tensor", axis=0, tiled=True)
    grad_gated = against_cols(grad_out_all, down_full)
    down_grad_part = across_rows(gated, grad_out_all)
    grad_both = jnp.stack([grad_gated * both[:, 1] * slope, grad_gated * activated], axis=1)
    grad_both_flat = grad_both.astype(jnp.bfloat16).reshape(seq_rows, 2 * local_hidden)
    in_grad_part = across_rows(ffn_in, grad_both_flat).reshape(model_dim, 2, local_hidden)
    grad_ffn_in = lax.psum_scatter(
        product_rows(grad_both_flat, in_flat, 1), "tensor", scatter_dimension=0, tiled=True
    )
    grad_second, second_gain_part = norm_backward(
        grad_ffn_in, second_normed, second_inv, norm_gains[1]
    )
    grad_middle = out_cotangent + grad_second
    middle_all = lax.all_gather(grad_middle.astype(jnp.bfloat16), "tensor", axis=0, tiled=True)
    out_grad_part = across_rows(mixed_flat, middle_all)
    grad_mixed = (
        against_cols(middle_all, out_full)
        .astype(jnp.bfloat16)
        .reshape(seq_rows, local_heads, head_dim)
    )
    deltas = jnp.sum(grad_mixed.astype(jnp.float32) * mixed_part.astype(jnp.float32), axis=-1)
    grad_kv_pad = jnp.zeros((seq_rows + 2 * reach, 2 * head_feats), jnp.float32)
    allowed = block_mask(query_ids, key_ids, reach)
    grad_q, grad_k, grad_v = block_backward(
        queries, keys_pad, values_pad, allowed, norm_part, grad_mixed, deltas
    )
    update = jnp.concatenate(
        [grad_k.reshape(span, head_feats), grad_v.reshape(span, head_feats)], axis=1
    )
    grad_kv_pad = grad_kv_pad.at[0:span].add(update)
    edge_grads = jnp.concatenate([grad_kv_pad[:reach], grad_kv_pad[seq_rows + reach :]], axis=0)
    edge_ext = padded(edge_grads.astype(jnp.bfloat16), (("dp", 0),), reach).astype(edge_grads.dtype)
    own_grads = grad_kv_pad[reach : reach + seq_rows]
    own_grads = own_grads.at[:reach].add(edge_ext[:reach])
    own_grads = own_grads.at[seq_rows - reach :].add(edge_ext[3 * reach :])
    grad_keys = own_grads[:, :head_feats].reshape(seq_rows, local_heads, head_dim)
    grad_values = own_grads[:, head_feats:].reshape(seq_rows, local_heads, head_dim)
    grad_proj = jnp.stack(
        [
            unrotate(grad_q, cos_table, sin_table),
            unrotate(grad_keys, cos_table, sin_table),
            grad_values,
        ],
        axis=2,
    )
    grad_proj_flat = grad_proj.astype(jnp.bfloat16).reshape(seq_rows, 3 * head_feats)
    qkv_grad_part = across_rows(normed_in, grad_proj_flat)
    grad_norm_in = lax.psum_scatter(
        product_rows(grad_proj_flat, qkv_full, 1).astype(jnp.bfloat16),
        "tensor",
        scatter_dimension=0,
        tiled=True,
    ).astype(jnp.float32)
    grad_first, first_gain_part = norm_backward(
        grad_norm_in, first_normed, first_inv, norm_gains[0]
    )
    residual_grad = grad_middle + grad_first
    gains_grad = lax.psum(jnp.stack([first_gain_part, second_gain_part]), ("dp", "tensor"))
    qkv_grad, out_weight_grad, in_grad, down_grad = (
        lax.psum_scatter(
            qkv_grad_part.astype(jnp.bfloat16), "dp", scatter_dimension=0, tiled=True
        ).astype(jnp.float32),
        lax.psum_scatter(
            out_grad_part.astype(jnp.bfloat16), "dp", scatter_dimension=1, tiled=True
        ).astype(jnp.float32),
        lax.psum_scatter(
            in_grad_part.astype(jnp.bfloat16), "dp", scatter_dimension=0, tiled=True
        ).astype(jnp.float32),
        lax.psum_scatter(
            down_grad_part.astype(jnp.bfloat16), "dp", scatter_dimension=1, tiled=True
        ).astype(jnp.float32),
    )
    new_qkv, new_qkv_moments = adam_update(qkv_weight, qkv_moments, qkv_grad, DECAY_RATE)
    new_out, new_out_moments = adam_update(out_weight, out_moments, out_weight_grad, DECAY_RATE)
    new_in, new_in_moments = adam_update(in_weight, in_moments, in_grad, DECAY_RATE)
    new_down, new_down_moments = adam_update(down_weight, down_moments, down_grad, DECAY_RATE)
    new_gains, new_gain_moments = adam_update(norm_gains, gain_moments, gains_grad, 0.0)
    return (
        block_out,
        residual_grad,
        qkv_grad,
        out_weight_grad,
        in_grad,
        down_grad,
        gains_grad,
        new_qkv,
        new_out,
        new_in,
        new_down,
        new_gains,
        new_qkv_moments,
        new_out_moments,
        new_in_moments,
        new_down_moments,
        new_gain_moments,
    )


def solution(mesh):
    return jax.shard_map(
        local,
        mesh=mesh,
        in_specs=(
            P(("dp", "tensor"), None),
            P(("dp", "tensor"), None),
            P(),
            P("dp", "tensor"),
            P("tensor", "dp"),
            P("dp", None, "tensor"),
            P("tensor", "dp"),
            P(),
            P(None, "dp", "tensor"),
            P(None, "tensor", "dp"),
            P(None, "dp", None, "tensor"),
            P(None, "tensor", "dp"),
            P(),
        ),
        out_specs=(
            P(("dp", "tensor"), None),
            P(("dp", "tensor"), None),
            P("dp", "tensor"),
            P("tensor", "dp"),
            P("dp", None, "tensor"),
            P("tensor", "dp"),
            P(),
            P("dp", "tensor"),
            P("tensor", "dp"),
            P("dp", None, "tensor"),
            P("tensor", "dp"),
            P(),
            P(None, "dp", "tensor"),
            P(None, "tensor", "dp"),
            P(None, "dp", None, "tensor"),
            P(None, "tensor", "dp"),
            P(),
        ),
        check_vma=False,
    )
```

profile of v0, /device:TPU:0, one launch (start us, length us, event | category | flops | bytes accessed | tf_op | source)
XLA Modules:
  0.0 751.8 jit_solution(12880494471490557528)
XLA Ops:
  15.8 20.5 %all-gather.9.cloned.1.call-done = bf16[512,1024]{1,0:T(8,128)(2,1)} async-done(((bf16[256,1024]{1,0:T(8,128)(2,1)}), bf16[512,1024]{1,0:T(8,128)(2,1)}) %all-gather.9.cloned.1.call-update) | async-done | bytes 1048592 | tf_op jit(solution)/shard_map/all_gather | solution.py:218
  36.2 48.3 %all-gather.11.cloned.1.call-done = bf16[1024,1536]{1,0:T(8,128)(2,1)} async-done(((bf16[64,1536]{1,0:T(8,128)(2,1)}), bf16[1024,1536]{1,0:T(8,128)(2,1)}) %all-gather.11.cloned.1.call-update) | async-done | bytes 3145744 | tf_op jit(solution)/shard_map/all_gather | solution.py:199
  84.6 4.1 fusion.67
  106.3 18.5 %all-gather.13.cloned.1.call-done = bf16[512,1024]{0,1:T(8,128)(2,1)} async-done(((bf16[512,64]{0,1:T(8,128)(2,1)}), bf16[512,1024]{0,1:T(8,128)(2,1)}) %all-gather.13.cloned.1.call-update) | async-done | bytes 1048592 | tf_op jit(solution)/shard_map/all_gather | solution.py:200
  124.8 3.4 fusion.68
  129.4 29.9 %reduce-scatter.9.cloned.1.call-done = f32[256,1024]{1,0:T(8,128)} async-done(((f32[512,1024]{1,0:T(8,128)}), f32[256,1024]{1,0:T(8,128)}) %reduce-scatter.9.cloned.1.call-update) | async-done | bytes 1048592 | tf_op jit(solution)/shard_map/reduce_scatter | solution.py:234
  163.0 57.7 %all-gather.17.cloned.1.call-done = bf16[1024,2,1312]{2,0,1:T(8,128)(2,1)} async-done(((bf16[64,2,1312]{2,0,1:T(8,128)(2,1)}), bf16[1024,2,1312]{2,0,1:T(8,128)(2,1)}) %all-gather.17.cloned.1.call-update) | async-done | bytes 5373968 | tf_op jit(solution)/shard_map/all_gather | solution.py:201
  220.7 8.1 %copy.60 = bf16[1024,2,1312]{0,2,1:T(8,128)(2,1)} copy(bf16[1024,2,1312]{2,0,1:T(8,128)(2,1)} %all-gather.17.cloned.1.call-done) | data formatting | bytes 10747904 | tf_op jit(solution)/shard_map/all_gather | solution.py:201
  228.8 13.8 %all-gather.15.cloned.1.call-done = bf16[512,1024]{1,0:T(8,128)(2,1)} async-done(((bf16[256,1024]{1,0:T(8,128)(2,1)}), bf16[512,1024]{1,0:T(8,128)(2,1)}) %all-gather.15.cloned.1.call-update) | async-done | bytes 1048592 | tf_op jit(solution)/shard_map/all_gather | solution.py:239
  242.6 5.3 fusion.2
  252.0 14.1 %all-gather.21.cloned.1.call-done = bf16[512,1024]{1,0:T(8,128)(2,1)} async-done(((bf16[256,1024]{1,0:T(8,128)(2,1)}), bf16[512,1024]{1,0:T(8,128)(2,1)}) %all-gather.21.cloned.1.call-update) | async-done | bytes 1048592 | tf_op jit(solution)/shard_map/all_gather | solution.py:252
  266.1 5.1 convolution_convert_fusion.1
  271.2 65.3 %reduce-scatter.23.cloned.1.call-done = bf16[1312,64]{0,1:T(8,128)(2,1)} async-done(((bf16[1312,1024]{0,1:T(8,128)(2,1)}), bf16[1312,64]{0,1:T(8,128)(2,1)}) %reduce-scatter.23.cloned.1.call-update) | async-done | bytes 167952 | tf_op jit(solution)/shard_map/reduce_scatter | solution.py:320
  341.7 43.1 %all-gather.19.cloned.1.call-done = bf16[1312,1024]{0,1:T(8,128)(2,1)} async-done(((bf16[1312,64]{0,1:T(8,128)(2,1)}), bf16[1312,1024]{0,1:T(8,128)(2,1)}) %all-gather.19.cloned.1.call-update) | async-done | bytes 2686992 | tf_op jit(solution)/shard_map/all_gather | solution.py:202
  384.7 6.5 fusion.9
  392.7 7.2 convolution_bitcast_fusion
  400.4 5.0 convolution_convert_fusion.4
  405.5 25.1 %reduce-scatter.13.cloned.1.call-done = f32[256,1024]{1,0:T(8,128)} async-done(((f32[512,1024]{1,0:T(8,128)}), f32[256,1024]{1,0:T(8,128)}) %reduce-scatter.13.cloned.1.call-update) | async-done | bytes 1048592 | tf_op jit(solution)/shard_map/reduce_scatter | solution.py:258
  432.9 20.9 %reduce-scatter.11.cloned.1.call-done = bf16[256,1024]{1,0:T(8,128)(2,1)} async-done(((bf16[512,1024]{1,0:T(8,128)(2,1)}), bf16[256,1024]{1,0:T(8,128)(2,1)}) %reduce-scatter.11.cloned.1.call-update) | async-done | bytes 524304 | tf_op jit(solution)/shard_map/reduce_scatter | solution.py:245
  453.9 3.3 fusion.60
  457.3 21.4 %all-gather.23.cloned.1.call-done = bf16[512,1024]{1,0:T(8,128)(2,1)} async-done(((bf16[256,1024]{1,0:T(8,128)(2,1)}), bf16[512,1024]{1,0:T(8,128)(2,1)}) %all-gather.23.cloned.1.call-update) | async-done | bytes 1048592 | tf_op jit(solution)/shard_map/all_gather | solution.py:265
  481.1 5.6 fusion.57
  486.8 6.7 multiply_convert_fusion
  512.1 3.7 scatter-add.6
  517.2 3.3 scatter-add.9
  529.7 6.4 convolution_convert_fusion
  537.4 5.0 convolution_convert_fusion.2
  545.7 19.0 %reduce-scatter.19.cloned.1.call-done = bf16[512,64]{0,1:T(8,128)(2,1)} async-done(((bf16[512,1024]{0,1:T(8,128)(2,1)}), bf16[512,64]{0,1:T(8,128)(2,1)}) %reduce-scatter.19.cloned.1.call-update) | async-done | bytes 65552 | tf_op jit(solution)/shard_map/reduce_scatter | solution.py:314
  568.2 18.6 %reduce-scatter.15.cloned.1.call-done = bf16[256,1024]{1,0:T(8,128)(2,1)} async-done(((bf16[512,1024]{1,0:T(8,128)(2,1)}), bf16[256,1024]{1,0:T(8,128)(2,1)}) %reduce-scatter.15.cloned.1.call-update) | async-done | bytes 524304 | tf_op jit(solution)/shard_map/reduce_scatter | solution.py:299
  590.2 40.3 %psum.7 = f32[2,1024]{1,0:T(2,128)} all-reduce(f32[2,1024]{1,0:T(2,128)} %pad_maximum_fusion.12), channel_id=1, replica_groups=mesh['dp'=16,'tensor'=2] {'dp','tensor'}, use_global_device_ids=true, to_apply=%region_25.26 | all-reduce | flops 2048 | bytes 16384 | tf_op jit(solution)/shard_map/psum | solution.py:309
  636.3 36.3 %reduce-scatter.21.cloned.1.call-done = bf16[64,2,1312]{2,0,1:T(8,128)(2,1)} async-done(((bf16[1024,2,1312]{2,0,1:T(8,128)(2,1)}), bf16[64,2,1312]{2,0,1:T(8,128)(2,1)}) %reduce-scatter.21.cloned.1.call-update) | async-done | bytes 335888 | tf_op jit(solution)/shard_map/reduce_scatter | solution.py:317
  679.4 62.6 %reduce-scatter.17.cloned.1.call-done = bf16[64,1536]{1,0:T(8,128)(2,1)} async-done(((bf16[1024,1536]{1,0:T(8,128)(2,1)}), bf16[64,1536]{1,0:T(8,128)(2,1)}) %reduce-scatter.17.cloned.1.call-update) | async-done | bytes 196624 | tf_op jit(solution)/shard_map/reduce_scatter | solution.py:311
  (217 shorter events, 102.6 us)
Async XLA Ops:
  7.2 29.0 %all-gather.9.cloned.1.call-start = ((), (), s32[]{:S(2)}) async-start(), calls=%async_computation.8 | async-start | bytes 1572864 | tf_op jit(solution)/shard_map/all_gather | solution.py:218
  10.2 78.4 %copy-start.37 = (f32[256]{0:T(256)}, f32[256]{0:T(256)S(1)}, u32[]{:S(2)}) copy-start(f32[256]{0:T(256)S(1)} %add_rsqrt_fusion.1) | copy-start | bytes 3076
  12.1 72.5 %all-gather.11.cloned.1.call-start = ((), (), s32[]{:S(2)}) async-start(), calls=%async_computation.9 | async-start | bytes 3342336 | tf_op jit(solution)/shard_map/all_gather | solution.py:199
  12.9 112.0 %all-gather.13.cloned.1.call-start = ((), (), s32[]{:S(2)}) async-start(), calls=%async_computation.10 | async-start | bytes 1114112 | tf_op jit(solution)/shard_map/all_gather | solution.py:200
  13.6 145.7 %reduce-scatter.9.cloned.1.call-start = ((), (), s32[]{:S(2)}) async-start(), calls=%async_computation.11 | async-start | bytes 3145728 | tf_op jit(solution)/shard_map/reduce_scatter | solution.py:234
  15.0 74.9 %copy-start.15 = (f32[512,64]{0,1:T(8,128)}, f32[512,64]{0,1:T(8,128)S(1)}, u32[]{:S(2)}) copy-start(f32[512,64]{0,1:T(8,128)S(1)} %get-tuple-element.165) | copy-start | bytes 393220
  15.7 73.8 %copy-start.26 = (f32[512,64]{0,1:T(8,128)}, f32[512,64]{0,1:T(8,128)S(1)}, u32[]{:S(2)}) copy-start(f32[512,64]{0,1:T(8,128)S(1)} %get-tuple-element.167) | copy-start | bytes 393220
  90.3 3.9 collective-permute-start
  92.5 3.4 collective-permute-start.1
  106.3 22.0 %copy-start.31 = (bf16[8,64,512]{2,1,0:T(8,128)(2,1)}, bf16[8,64,512]{2,1,0:T(8,128)(2,1)S(1)}, u32[]{:S(2)}) copy-start(bf16[8,64,512]{2,1,0:T(8,128)(2,1)S(1)} %convolution_convert_fusion.7) | copy-start | bytes 1572868
  128.2 92.5 %all-gather.17.cloned.1.call-start = ((), (), s32[]{:S(2)}) async-start(), calls=%async_computation.13 | async-start | bytes 6127616 | tf_op jit(solution)/shard_map/all_gather | solution.py:201
  129.3 32.7 %copy-start.10 = (f32[256,1024]{1,0:T(8,128)S(1)}, f32[256,1024]{1,0:T(8,128)}, u32[]{:S(2)}) copy-start(f32[256,1024]{1,0:T(8,128)} %param.22) | copy-start | bytes 3145732
  129.3 113.3 %all-gather.15.cloned.1.call-start = ((), (), s32[]{:S(2)}) async-start(), calls=%async_computation.12 | async-start | bytes 1572864 | tf_op jit(solution)/shard_map/all_gather | solution.py:239
  162.0 104.1 %all-gather.21.cloned.1.call-start = ((), (), s32[]{:S(2)}) async-start(), calls=%async_computation.16 | async-start | bytes 1572864 | tf_op jit(solution)/shard_map/all_gather | solution.py:252
  162.9 173.6 %reduce-scatter.23.cloned.1.call-start = ((), (), s32[]{:S(2)}) async-start(), calls=%async_computation.23 | async-start | bytes 3063808 | tf_op jit(solution)/shard_map/reduce_scatter | solution.py:320
  271.2 113.6 %all-gather.19.cloned.1.call-start = ((), (), s32[]{:S(2)}) async-start(), calls=%async_computation.14 | async-start | bytes 3063808 | tf_op jit(solution)/shard_map/all_gather | solution.py:202
  341.6 89.0 %reduce-scatter.13.cloned.1.call-start = ((), (), s32[]{:S(2)}) async-start(), calls=%async_computation.17 | async-start | bytes 3145728 | tf_op jit(solution)/shard_map/reduce_scatter | solution.py:258
  400.0 53.9 %reduce-scatter.11.cloned.1.call-start = ((), (), s32[]{:S(2)}) async-start(), calls=%async_computation.15 | async-start | bytes 1572864 | tf_op jit(solution)/shard_map/reduce_scatter | solution.py:245
  405.5 73.2 %all-gather.23.cloned.1.call-start = ((), (), s32[]{:S(2)}) async-start(), calls=%async_computation.18 | async-start | bytes 1572864 | tf_op jit(solution)/shard_map/all_gather | solution.py:265
  457.2 107.5 %reduce-scatter.19.cloned.1.call-start = ((), (), s32[]{:S(2)}) async-start(), calls=%async_computation.21 | async-start | bytes 1114112 | tf_op jit(solution)/shard_map/reduce_scatter | solution.py:314
  486.8 11.7 %copy-start.2 = (f32[8,64,640]{2,1,0:T(8,128)}, f32[8,64,640]{2,1,0:T(8,128)S(1)}, u32[]{:S(2)}) copy-start(f32[8,64,640]{2,1,0:T(8,128)S(1)} %fusion.57) | copy-start | bytes 3932164
  499.5 10.0 %collective-permute-start.2 = (bf16[64,1024]{0,1:T(8,128)(2,1)}, bf16[64,1024]{0,1:T(8,128)(2,1)}, u32[]{:S(2)}, u32[]{:S(2)}) collective-permute-start(bf16[64,1024]{0,1:T(8,128)(2,1)} %get-tuple-element.137), channel_id=1, source_target_pairs={{0,2},{2,4},{4,6},{6,8},{8,10},{10,12},{12,14},{14,16},{16,18},{18... | collective-permute-start | bytes 393224 | tf_op jit(solution)/shard_map/ppermute | solution.py:30
  501.8 7.7 %collective-permute-start.3 = (bf16[64,1024]{0,1:T(8,128)(2,1)}, bf16[64,1024]{0,1:T(8,128)(2,1)}, u32[]{:S(2)}, u32[]{:S(2)}) collective-permute-start(bf16[64,1024]{0,1:T(8,128)(2,1)} %get-tuple-element.138), channel_id=1, source_target_pairs={{2,0},{4,2},{6,4},{8,6},{10,8},{12,10},{14,12},{16,14},{18,16},{20... | collective-permute-start | bytes 393224 | tf_op jit(solution)/shard_map/ppermute | solution.py:31
  505.0 81.8 %reduce-scatter.15.cloned.1.call-start = ((), (), s32[]{:S(2)}) async-start(), calls=%async_computation.19 | async-start | bytes 1572864 | tf_op jit(solution)/shard_map/reduce_scatter | solution.py:299
  515.8 7.4 copy-start.27
  529.7 142.9 %reduce-scatter.21.cloned.1.call-start = ((), (), s32[]{:S(2)}) async-start(), calls=%async_computation.22 | async-start | bytes 6127616 | tf_op jit(solution)/shard_map/reduce_scatter | solution.py:317
  536.2 205.8 %reduce-scatter.17.cloned.1.call-start = ((), (), s32[]{:S(2)}) async-start(), calls=%async_computation.20 | async-start | bytes 3342336 | tf_op jit(solution)/shard_map/reduce_scatter | solution.py:311
  544.8 85.8 %copy-start.36 = (f32[2,1024]{1,0:T(2,128)S(1)}, f32[2,1024]{1,0:T(2,128)}, u32[]{:S(2)}) copy-start(f32[2,1024]{1,0:T(2,128)} %param.28) | copy-start | bytes 24580
  544.8 89.1 %copy-start.9 = (f32[256,1024]{1,0:T(8,128)S(1)}, f32[256,1024]{1,0:T(8,128)}, u32[]{:S(2)}) copy-start(f32[256,1024]{1,0:T(8,128)} %get-tuple-element.127) | copy-start | bytes 3145732
  568.2 104.4 %copy-start.13 = (f32[64,2,1312]{2,1,0:T(2,128)S(1)}, f32[64,2,1312]{2,1,0:T(2,128)}, u32[]{:S(2)}) copy-start(f32[64,2,1312]{2,1,0:T(2,128)} %param.26) | copy-start | bytes 2015236
  674.5 67.5 %copy-start.17 = (f32[2,64,1536]{2,1,0:T(8,128)S(1)}, f32[2,64,1536]{2,1,0:T(8,128)}, u32[]{:S(2)}) copy-start(f32[2,64,1536]{2,1,0:T(8,128)} %param.29) | copy-start | bytes 2359300
  674.5 68.5 %copy-start.20 = (f32[64,1536]{1,0:T(8,128)S(1)}, f32[64,1536]{1,0:T(8,128)}, u32[]{:S(2)}) copy-start(f32[64,1536]{1,0:T(8,128)} %param.24) | copy-start | bytes 1179652
  (34 other events, 114.0 us)
Sparse Core Ops, SparseCore 0:
  12.2 23.9 all-gather.8
  39.1 45.4 all-gather.10
  87.3 37.4 all-gather.12
  128.4 30.8 reduce-scatter.8
  162.0 58.6 all-gather.16
  222.7 19.9 all-gather.14
  244.7 21.2 all-gather.20
  271.3 65.1 reduce-scatter.22
  341.7 42.9 all-gather.18
  400.1 30.5 reduce-scatter.12
  433.5 20.3 reduce-scatter.10
  457.3 21.2 all-gather.22
  505.1 59.5 reduce-scatter.18
  567.4 19.3 reduce-scatter.14
  590.5 82.0 reduce-scatter.20
  676.3 65.6 reduce-scatter.16
where the time goes:
time: 762 us; the launch traced here: 752 us
  waiting for transfers between devices  517 us (68%)
  matrix products  76.6 us (10%)
  other arithmetic  56 us (7%)
  blocking collectives  40.3 us (5%)
  local copies, waits for them, and re-layouts  38.4 us (5%)
  between operations  15 us (2%)
  starting transfers between devices  8.46 us (1%)
    reduce_scatter x1, waiting for transfers between devices, local(): lax.psum_scatter(down_grad_part.astype(jnp.bfloat16), 'dp', scatter_dimen...  65.3 us
    reduce_scatter x1, waiting for transfers between devices, local(): lax.psum_scatter(qkv_grad_part.astype(jnp.bfloat16), 'dp', scatter_dimens...  62.6 us
    all_gather x1, waiting for transfers between devices, local(): lax.all_gather(in_weight.astype(jnp.bfloat16), 'dp', axis=0, tiled=True)  57.7 us
    all_gather x1, waiting for transfers between devices, local(): lax.all_gather(qkv_weight.astype(jnp.bfloat16), 'dp', axis=0, tiled=True)  48.3 us
    all_gather x1, waiting for transfers between devices, local(): lax.all_gather(down_weight.astype(jnp.bfloat16), 'dp', axis=1, tiled=True)  43.1 us
    psum x1, blocking collectives, local(): lax.psum(jnp.stack([first_gain_part, second_gain_part]), ('dp', 'tensor'))  40.3 us
    reduce_scatter x1, waiting for transfers between devices, local(): lax.psum_scatter(in_grad_part.astype(jnp.bfloat16), 'dp', scatter_dimensi...  36.3 us
    reduce_scatter x1, waiting for transfers between devices, local(): lax.psum_scatter(product_rows(mixed_flat, out_full, 0), 'tensor', scatter...  29.9 us
  transfers between devices with their start and end apart: 20, of which 17 were waited for; matrix products, arithmetic and copies ran while one was open for 14% of the time, Pallas kernels for 0%

commit v1 on v0

--- a/solution.py
+++ b/solution.py
@@ -1,8 +1,11 @@
+import functools
 import math
 
 import jax
 import jax.numpy as jnp
 from jax import lax
+from jax.experimental import pallas as pl
+from jax.experimental.pallas import tpu as pltpu
 from jax.sharding import PartitionSpec as P
 
 HD = 64
@@ -18,6 +21,140 @@
 LEARN_RATE = 0.005
 DECAY_RATE = 0.1
 MASKED = -1e30
+
+MESH = pl.DeviceIdType.MESH
+DEPTH, SIDES, CORES = 4, 2, 2
+DIRECT = 3
+
+
+def gather_kernel(count, *refs):
+    shards, fulls = refs[:count], refs[count : 2 * count]
+    own_sem, z_send, z_recv, y_send, y_recv, c_send, c_recv = refs[2 * count :]
+    me = lax.axis_index("dp")
+    z, y, c = me // 4, (me // 2) % 2, me % 2
+    z_peers = [lax.rem(z + d, DEPTH) * 4 + y * 2 + c for d in range(1, DEPTH)]
+    y_peer = z * 4 + (1 - y) * 2 + c
+    c_peer = z * 4 + y * 2 + (1 - c)
+
+    barrier = pltpu.get_barrier_semaphore()
+    for peer in z_peers + [y_peer, c_peer]:
+        pl.semaphore_signal(barrier, inc=1, device_id={"dp": peer}, device_id_type=MESH)
+    pl.semaphore_wait(barrier, DEPTH + 1)
+
+    def block(i, d, side):
+        rows = shards[i].shape[0]
+        origin = lax.rem(z - d + DEPTH, DEPTH) * 4 + (y if side == 0 else 1 - y) * 2 + c
+        return fulls[i].at[pl.ds(pl.multiple_of(origin * rows, rows), rows), :]
+
+    def send(src, dst, sem_s, sem_r, peer):
+        copy = pltpu.make_async_remote_copy(
+            src_ref=src,
+            dst_ref=dst,
+            send_sem=sem_s,
+            recv_sem=sem_r,
+            device_id={"dp": peer},
+            device_id_type=MESH,
+        )
+        copy.start()
+        return copy
+
+    own, z_copies, y_copies, c_copies = [], {}, {}, {}
+    for i in range(count):
+        own.append(pltpu.make_async_copy(shards[i], block(i, 0, 0), own_sem.at[i]))
+        own[-1].start()
+        for d in range(1, DEPTH):
+            z_copies[i, d] = send(
+                shards[i], block(i, 0, 0), z_send.at[i, d - 1], z_recv.at[i, d - 1], z_peers[d - 1]
+            )
+        y_copies[i, 0] = send(shards[i], block(i, 0, 0), y_send.at[i, 0], y_recv.at[i, 0], y_peer)
+        c_copies[i, 0] = send(shards[i], block(i, 0, 0), c_send.at[i, 0], c_recv.at[i, 0], c_peer)
+    for i in range(count):
+        for d in range(1, DEPTH):
+            z_copies[i, d].wait_recv()
+            here = block(i, d, 0)
+            y_copies[i, d] = send(here, here, y_send.at[i, d], y_recv.at[i, d], y_peer)
+            c_copies[i, 2 * d] = send(here, here, c_send.at[i, 2 * d], c_recv.at[i, 2 * d], c_peer)
+    for i in range(count):
+        for d in range(DEPTH):
+            y_copies[i, d].wait_recv()
+            here = block(i, d, 1)
+            k = 2 * d + 1
+            c_copies[i, k] = send(here, here, c_send.at[i, k], c_recv.at[i, k], c_peer)
+    for i in range(count):
+        for k in range(2 * DEPTH):
+            c_copies[i, k].wait_recv()
+    for copy in own:
+        copy.wait()
+    for table in (z_copies, y_copies, c_copies):
+        for copy in table.values():
+            copy.wait_send()
+
+
+def gather_all(*shards):
+    count = len(shards)
+    total = sum(math.prod(s.shape) for s in shards) * 2
+    return pl.pallas_call(
+        functools.partial(gather_kernel, count),
+        out_shape=[
+            jax.ShapeDtypeStruct((s.shape[0] * DEPTH * SIDES * CORES, s.shape[1]), s.dtype)
+            for s in shards
+        ],
+        in_specs=[pl.BlockSpec(memory_space=pltpu.VMEM)] * count,
+        out_specs=[pl.BlockSpec(memory_space=pl.ANY)] * count,
+        scratch_shapes=[
+            pltpu.SemaphoreType.DMA((count,)),
+            pltpu.SemaphoreType.DMA((count, 3)),
+            pltpu.SemaphoreType.DMA((count, 3)),
+            pltpu.SemaphoreType.DMA((count, 4)),
+            pltpu.SemaphoreType.DMA((count, 4)),
+            pltpu.SemaphoreType.DMA((count, 8)),
+            pltpu.SemaphoreType.DMA((count, 8)),
+        ],
+        compiler_params=pltpu.CompilerParams(
+            collective_id=1, has_side_effects=True, vmem_limit_bytes=8 << 20
+        ),
+        cost_estimate=pl.CostEstimate(flops=0, bytes_accessed=total * 200, transcendentals=0),
+    )(*shards)
+
+
+def sum_everywhere(value):
+    for axis in ("tensor", "dp"):
+        size, step = lax.axis_size(axis), 1
+        if size & (size - 1):
+            value = lax.psum(value, axis)
+            continue
+        while step < size:
+            value = value + lax.ppermute(value, axis, [(i, i ^ step) for i in range(size)])
+            step *= 2
+    return value
+
+
+def gather_tokens(value):
+    size = lax.axis_size("tensor")
+    if size != 2:
+        return lax.all_gather(value, "tensor", axis=0, tiled=True)
+    rows = value.shape[0]
+    index = lax.axis_index("tensor")
+    other = lax.ppermute(value, "tensor", [(0, 1), (1, 0)])
+    whole = jnp.zeros((2 * rows,) + value.shape[1:], value.dtype)
+    whole = lax.dynamic_update_slice_in_dim(whole, value, index * rows, 0)
+    return lax.dynamic_update_slice_in_dim(whole, other, (1 - index) * rows, 0)
+
+
+def scatter_tokens(left, multiply):
+    size = lax.axis_size("tensor")
+    if size != 2:
+        part = multiply(left).astype(jnp.bfloat16)
+        return lax.psum_scatter(part, "tensor", scatter_dimension=0, tiled=True).astype(
+            jnp.float32
+        )
+    rows = left.shape[0] // 2
+    index = lax.axis_index("tensor")
+    theirs = lax.dynamic_slice_in_dim(left, (1 - index) * rows, rows, 0)
+    ours = lax.dynamic_slice_in_dim(left, index * rows, rows, 0)
+    sent = multiply(theirs).astype(jnp.bfloat16)
+    got = lax.ppermute(sent, "tensor", [(0, 1), (1, 0)])
+    return multiply(ours) + got.astype(jnp.float32)
 
 
 def padded(value, sides, width):
@@ -195,18 +332,25 @@
     reach = HALF_WIN
     block_rows = min(512, seq_rows)
     span = block_rows + 2 * reach
-    qkv_full, out_full, in_full, down_full = (
-        lax.all_gather(qkv_weight.astype(jnp.bfloat16), "dp", axis=0, tiled=True),
-        lax.all_gather(out_weight.astype(jnp.bfloat16), "dp", axis=1, tiled=True),
-        lax.all_gather(in_weight.astype(jnp.bfloat16), "dp", axis=0, tiled=True),
-        lax.all_gather(down_weight.astype(jnp.bfloat16), "dp", axis=1, tiled=True),
-    )
+    cast = lambda w: w.astype(jnp.bfloat16)
+    shards = [
+        cast(qkv_weight),
+        cast(out_weight).T,
+        cast(in_weight[:, 0]),
+        cast(in_weight[:, 1]),
+        cast(down_weight).T,
+    ]
+    grad_out_all = gather_tokens(out_cotangent.astype(jnp.bfloat16))
+    first_normed, first_inv, first_scaled = norm_forward(residual_in, norm_gains[0])
+    normed_in = gather_tokens(first_scaled.astype(jnp.bfloat16))
+    direct = DIRECT if (data_count, tensor_count) == (16, 2) else 0
+    fulls = list(gather_all(*shards[:direct])) if direct else []
+    fulls += [lax.all_gather(w, "dp", axis=0, tiled=True) for w in shards[direct:]]
+    qkv_full, out_full, act_full, gate_full, down_full = fulls
     model_dim = qkv_full.shape[0]
     head_dim = HD
     local_heads = qkv_full.shape[1] // (3 * head_dim)
-    local_hidden = in_full.shape[2]
     head_feats = local_heads * head_dim
-    in_flat = in_full.reshape(model_dim, 2 * local_hidden)
     first_token = lax.axis_index("dp") * seq_rows
     places = first_token + jnp.arange(seq_rows, dtype=jnp.int32)
     query_ids, offsets = seq_coords(seq_lengths, places)
@@ -214,8 +358,6 @@
     key_places = first_token - reach + jnp.arange(seq_rows + 2 * reach, dtype=jnp.int32)
     inside = (key_places >= 0) & (key_places < seq_rows * data_count)
     key_ids = jnp.where(inside, seq_coords(seq_lengths, key_places)[0], -1)
-    first_normed, first_inv, first_scaled = norm_forward(residual_in, norm_gains[0])
-    normed_in = lax.all_gather(first_scaled.astype(jnp.bfloat16), "tensor", axis=0, tiled=True)
     proj = jnp.dot(normed_in, qkv_full, preferred_element_type=jnp.float32).reshape(
         seq_rows, local_heads, 3, head_dim
     )
@@ -231,41 +373,54 @@
     allowed = block_mask(query_ids, key_ids, reach)
     mixed_part, norm_part = block_forward(queries, keys_pad, values_pad, allowed)
     mixed_flat = mixed_part.reshape(seq_rows, head_feats)
-    attn_out = lax.psum_scatter(
-        product_rows(mixed_flat, out_full, 0), "tensor", scatter_dimension=0, tiled=True
-    )
+    attn_out = scatter_tokens(mixed_flat, lambda r: against_cols(r, out_full))
     middle = residual_in + attn_out
     second_normed, second_inv, second_scaled = norm_forward(middle, norm_gains[1])
-    ffn_in = lax.all_gather(second_scaled.astype(jnp.bfloat16), "tensor", axis=0, tiled=True)
-    both = jnp.dot(ffn_in, in_flat, preferred_element_type=jnp.float32).reshape(
-        seq_rows, 2, local_hidden
-    )
-    activated, slope = gelu_parts(both[:, 0])
-    gated = (activated * both[:, 1]).astype(jnp.bfloat16)
-    ffn_out = lax.psum_scatter(
-        product_rows(gated, down_full, 0).astype(jnp.bfloat16),
-        "tensor",
-        scatter_dimension=0,
-        tiled=True,
-    ).astype(jnp.float32)
+    ffn_in = gather_tokens(second_scaled.astype(jnp.bfloat16))
+    act_pre = jnp.dot(ffn_in, act_full, preferred_element_type=jnp.float32)
+    gate = jnp.dot(ffn_in, gate_full, preferred_element_type=jnp.float32)
+    activated, slope = gelu_parts(act_pre)
+    gated = (activated * gate).astype(jnp.bfloat16)
+    grad_gated = jnp.dot(grad_out_all, down_full, preferred_element_type=jnp.float32)
+    grad_act = (grad_gated * gate * slope).astype(jnp.bfloat16)
+    grad_gate = (grad_gated * activated).astype(jnp.bfloat16)
+    if tensor_count == 2:
+        own = lax.axis_index("tensor")
+        near = lambda v, at: lax.dynamic_slice_in_dim(v, at * local_rows, local_rows, 0)
+        back = lambda at: against_cols(near(grad_act, at), act_full) + against_cols(
+            near(grad_gate, at), gate_full
+        )
+        sent = back(1 - own).astype(jnp.bfloat16)
+        got = lax.ppermute(sent, "tensor", [(0, 1), (1, 0)])
+        grad_ffn_in = back(own) + got.astype(jnp.float32)
+    else:
+        grad_ffn_in = lax.psum_scatter(
+            (against_cols(grad_act, act_full) + against_cols(grad_gate, gate_full)).astype(
+                jnp.bfloat16
+            ), "tensor", scatter_dimension=0, tiled=True
+        ).astype(jnp.float32)
+    ffn_parts = jnp.concatenate(
+        [
+            across_rows(grad_out_all, gated).astype(jnp.bfloat16),
+            across_rows(ffn_in, grad_act).astype(jnp.bfloat16),
+            across_rows(ffn_in, grad_gate).astype(jnp.bfloat16),
+        ],
+        axis=1,
+    )
+    grad_ffn_in, ffn_parts = lax.optimization_barrier((grad_ffn_in, ffn_parts))
+    ffn_grads = lax.psum_scatter(ffn_parts, "dp", scatter_dimension=0, tiled=True).astype(
+        jnp.float32
+    )
+    ffn_out = scatter_tokens(gated, lambda r: against_cols(r, down_full))
     block_out = middle + ffn_out
-    grad_out_all = lax.all_gather(out_cotangent.astype(jnp.bfloat16), "tensor", axis=0, tiled=True)
-    grad_gated = against_cols(grad_out_all, down_full)
-    down_grad_part = across_rows(gated, grad_out_all)
-    grad_both = jnp.stack([grad_gated * both[:, 1] * slope, grad_gated * activated], axis=1)
-    grad_both_flat = grad_both.astype(jnp.bfloat16).reshape(seq_rows, 2 * local_hidden)
-    in_grad_part = across_rows(ffn_in, grad_both_flat).reshape(model_dim, 2, local_hidden)
-    grad_ffn_in = lax.psum_scatter(
-        product_rows(grad_both_flat, in_flat, 1), "tensor", scatter_dimension=0, tiled=True
-    )
     grad_second, second_gain_part = norm_backward(
         grad_ffn_in, second_normed, second_inv, norm_gains[1]
     )
     grad_middle = out_cotangent + grad_second
-    middle_all = lax.all_gather(grad_middle.astype(jnp.bfloat16), "tensor", axis=0, tiled=True)
-    out_grad_part = across_rows(mixed_flat, middle_all)
+    middle_all = gather_tokens(grad_middle.astype(jnp.bfloat16))
+    out_grad_part = across_rows(middle_all, mixed_flat).astype(jnp.bfloat16)
     grad_mixed = (
-        against_cols(middle_all, out_full)
+        jnp.dot(middle_all, out_full, preferred_element_type=jnp.float32)
         .astype(jnp.bfloat16)
         .reshape(seq_rows, local_heads, head_dim)
     )
@@ -296,31 +451,22 @@
     )
     grad_proj_flat = grad_proj.astype(jnp.bfloat16).reshape(seq_rows, 3 * head_feats)
     qkv_grad_part = across_rows(normed_in, grad_proj_flat)
-    grad_norm_in = lax.psum_scatter(
-        product_rows(grad_proj_flat, qkv_full, 1).astype(jnp.bfloat16),
-        "tensor",
-        scatter_dimension=0,
-        tiled=True,
-    ).astype(jnp.float32)
+    attn_parts = jnp.concatenate([qkv_grad_part.astype(jnp.bfloat16), out_grad_part], axis=1)
+    attn_parts, ffn_grads = lax.optimization_barrier((attn_parts, ffn_grads))
+    hidden = gated.shape[1]
+    down_grad = ffn_grads[:, :hidden].T
+    in_grad = jnp.stack([ffn_grads[:, hidden : 2 * hidden], ffn_grads[:, 2 * hidden :]], axis=1)
+    attn_grads = lax.psum_scatter(attn_parts, "dp", scatter_dimension=0, tiled=True).astype(
+        jnp.float32
+    )
+    qkv_grad = attn_grads[:, : 3 * head_feats]
+    out_weight_grad = attn_grads[:, 3 * head_feats :].T
+    grad_norm_in = scatter_tokens(grad_proj_flat, lambda r: against_cols(r, qkv_full))
     grad_first, first_gain_part = norm_backward(
         grad_norm_in, first_normed, first_inv, norm_gains[0]
     )
     residual_grad = grad_middle + grad_first
-    gains_grad = lax.psum(jnp.stack([first_gain_part, second_gain_part]), ("dp", "tensor"))
-    qkv_grad, out_weight_grad, in_grad, down_grad = (
-        lax.psum_scatter(
-            qkv_grad_part.astype(jnp.bfloat16), "dp", scatter_dimension=0, tiled=True
-        ).astype(jnp.float32),
-        lax.psum_scatter(
-            out_grad_part.astype(jnp.bfloat16), "dp", scatter_dimension=1, tiled=True
-        ).astype(jnp.float32),
-        lax.psum_scatter(
-            in_grad_part.astype(jnp.bfloat16), "dp", scatter_dimension=0, tiled=True
-        ).astype(jnp.float32),
-        lax.psum_scatter(
-            down_grad_part.astype(jnp.bfloat16), "dp", scatter_dimension=1, tiled=True
-        ).astype(jnp.float32),
-    )
+    gains_grad = sum_everywhere(jnp.stack([first_gain_part, second_gain_part]))
     new_qkv, new_qkv_moments = adam_update(qkv_weight, qkv_moments, qkv_grad, DECAY_RATE)
     new_out, new_out_moments = adam_update(out_weight, out_moments, out_weight_grad, DECAY_RATE)
     new_in, new_in_moments = adam_update(in_weight, in_moments, in_grad, DECAY_RATE)

time: 762 us -> 402 us (0.53)
  waiting for transfers between devices: 517 us -> 113 us
  Pallas kernels: 0 us -> 65.4 us
  blocking collectives: 40.3 us -> 0 us
  local copies, waits for them, and re-layouts: 38.4 us -> 63.7 us
  starting transfers between devices: 8.46 us -> 29.4 us
  matrix products: 76.6 us -> 63.8 us
  other arithmetic: 56 us -> 46.1 us
    reduce_scatter x8 -> x1, waiting for transfers between devices: 278 us -> 14.2 us  [local(): lax.psum_scatter(attn_parts, 'dp', scatter_dimension=0, tiled=True)]
    all_gather x8 -> x2, waiting for transfers between devices: 237 us -> 0.01 us  [local(): lax.all_gather(w, 'dp', axis=0, tiled=True)]
    pallas_call x0 -> x1, Pallas kernels: none -> 65.4 us  [gather_all(): pl.pallas_call(functools.partial(gather_kernel, count), out_shape=[jax.Sh...]
    unnamed x16 -> x5, waiting for transfers between devices: 0.27 us -> 58.8 us
    psum x1 -> x0, blocking collectives: 40.3 us -> none  [local(): lax.psum(jnp.stack([first_gain_part, second_gain_part]), ('dp', 'tensor'))]
    ppermute x0 -> x13, waiting for transfers between devices: none -> 39.5 us  [the longest x4 24.4 us: gather_tokens(): other = lax.ppermute(value, 'tensor', [(0, 1), (1, 0)])]
    unnamed x96 -> x129, local copies, waits for them, and re-layouts: 15.7 us -> 42.4 us
    ppermute x0 -> x13, starting transfers between devices: none -> 15.2 us  [the longest x5 6.88 us: sum_everywhere(): lax.ppermute(value, axis, [(i, i ^ step) for i in range(size)])]
  transfers between devices with their start and end apart: 20 -> 21, of which waited for: 17 -> 11; matrix products, arithmetic and copies ran while one was open for 14% -> 34% of each run, Pallas kernels for 0% -> 17%
where the time goes in v1:
time: 402 us; the launch traced here: 396 us
  waiting for transfers between devices  113 us (28%)
  Pallas kernels  65.4 us (16%)
  matrix products  63.8 us (16%)
  local copies, waits for them, and re-layouts  63.7 us (16%)
  other arithmetic  46.1 us (11%)
  starting transfers between devices  29.4 us (7%)
  between operations  15.2 us (4%)
    pallas_call x1, Pallas kernels, gather_all(): pl.pallas_call(functools.partial(gather_kernel, count), out_shape=[jax.Sh...  65.4 us
    unnamed x5, waiting for transfers between devices  58.8 us
    unnamed x129, local copies, waits for them, and re-layouts  42.4 us
    ppermute x4, waiting for transfers between devices, gather_tokens(): other = lax.ppermute(value, 'tensor', [(0, 1), (1, 0)])  24.4 us
    dot_general x10, matrix products, against_cols(): lax.dot_general(left, right, (((1,), (1,)), ((), ())), preferred_element_...  19 us
    reduce_scatter x1, waiting for transfers between devices, local(): lax.psum_scatter(attn_parts, 'dp', scatter_dimension=0, tiled=True)  14.2 us
    ppermute x2, starting transfers between devices, padded(): before = lax.ppermute(last, axis, up)  11.4 us
    dot_general x5, matrix products, across_rows(): lax.dot_general(left, right, (((0,), (0,)), ((), ())), preferred_element_...  10.8 us
  transfers between devices with their start and end apart: 21, of which 11 were waited for; matrix products, arithmetic and copies ran while one was open for 34% of the time, Pallas kernels for 17%

profile of v1, /device:TPU:0, one launch (start us, length us, event | category | flops | bytes accessed | tf_op | source)
XLA Modules:
  0.0 396.3 jit_solution(229554677943060592)
XLA Ops:
  12.0 3.0 collective-permute-start
  16.5 65.4 %shard_map.265 = (bf16[1024,1536]{1,0:T(8,128)(2,1)S(1)}, bf16[1024,512]{1,0:T(8,128)(2,1)S(1)}, bf16[1024,1312]{1,0:T(8,128)(2,1)S(1)}) custom-call(bf16[64,1536]{1,0:T(8,128)(2,1)S(1)} %convert_element_type.146.refs_0_, bf16[64,512]{1,0:T(8,128)(2,1)S(1)} %convert_bitcast_fusion.1.refs_1_, bf16[64,1312]{1,0:T(8,128)(2,1)S(1)} %get-tuple-element.207.refs_2_), custom_call_target="tpu_custom_call" | custom-call | bytes 86016000 | tf_op jit(solution)/shard_map/pallas_call | solution.py:96
  86.1 3.1 fusion.105
  92.2 3.6 collective-permute-start.1
  99.8 2.6 exponential_reduce_fusion
  103.8 3.2 convolution_convert_fusion.9
  111.6 5.9 %collective-permute-done.3 = bf16[256,1024]{1,0:T(8,128)(2,1)S(1)} collective-permute-done((bf16[256,1024]{1,0:T(8,128)(2,1)S(1)}, bf16[256,1024]{1,0:T(8,128)(2,1)S(1)}, u32[]{:S(2)}, u32[]{:S(2)}) %collective-permute-start.3) | collective-permute-done | bytes 524320 | tf_op jit(solution)/shard_map/ppermute | solution.py:156
  119.2 9.5 %collective-permute-done.6 = bf16[256,1024]{1,0:T(8,128)(2,1)S(1)} collective-permute-done((bf16[256,1024]{1,0:T(8,128)(2,1)S(1)}, bf16[256,1024]{1,0:T(8,128)(2,1)S(1)}, u32[]{:S(2)}, u32[]{:S(2)}) %collective-permute-start.6) | collective-permute-done | bytes 524320 | tf_op jit(solution)/shard_map/ppermute | solution.py:138
  129.6 10.4 %collective-permute-done.4 = bf16[256,1024]{1,0:T(8,128)(2,1)S(1)} collective-permute-done((bf16[256,1024]{1,0:T(8,128)(2,1)S(1)}, bf16[256,1024]{1,0:T(8,128)(2,1)S(1)}, u32[]{:S(2)}, u32[]{:S(2)}) %collective-permute-start.4) | collective-permute-done | bytes 524320 | tf_op jit(solution)/shard_map/ppermute | solution.py:138
  140.0 3.1 fusion.106
  143.1 5.0 %fusion.6 = f32[512,1312]{0,1:T(8,128)} fusion(bf16[512,1024]{1,0:T(8,128)(2,1)S(1)} %constant_dynamic-update-slice_fusion.4, bf16[1024,1,1312]{2,0,1:T(8,128)(2,1)} %all-gather.6.cloned.1.call-done), kind=kOutput, calls=%fused_computation.22 | convolution fusion | flops 1375731712 | bytes 6422528 | tf_op jit(solution)/shard_map/dot_general | solution.py:381
  148.1 6.7 %multiply_convert_fusion.1 = (bf16[512,1312]{0,1:T(8,128)(2,1)S(1)}, bf16[512,1312]{0,1:T(8,128)(2,1)S(1)}, bf16[512,1312]{0,1:T(8,128)(2,1)S(1)}) fusion(f32[512,1312]{0,1:T(8,128)} %fusion.106, f32[512,1312]{0,1:T(8,128)} %fusion.6, bf16[512,1024]{1,0:T(8,128)(2,1)} %constant_dynamic-update-slice_fusion.2, bf16[1024,1312]{1,0:T(8,128)(2,1)} %all-gather.4.cloned.1.call-done), kind=kOutput, calls=%fused_computation.31 | convolution fusion | flops 1386479616 | bytes 13139968 | tf_op jit(solution)/shard_map/dot_general | solution.py:384
  162.3 2.8 convolution_convert_fusion.2
  165.1 4.2 %pad_maximum_fusion = bf16[1024,3936]{0,1:T(8,128)(2,1)} fusion(bf16[1024,1312]{0,1:T(8,128)(2,1)S(1)} %convolution_convert_fusion, bf16[1024,1312]{0,1:T(8,128)(2,1)S(1)} %convolution_convert_fusion.1, bf16[1024,1312]{0,1:T(8,128)(2,1)S(1)} %convolution_convert_fusion.2), kind=kLoop, calls=%fused_computation.5 | loop fusion | flops 24182784 | bytes 16121856 | tf_op jit(solution)/shard_map/concatenate | solution.py:402
  169.2 3.8 collective-permute-done.7
  174.1 10.9 %copy.111 = bf16[1024,3936]{1,0:T(8,128)(2,1)} copy(bf16[1024,3936]{0,1:T(8,128)(2,1)} %pad_maximum_fusion) | data formatting | bytes 16121856
  185.7 2.9 constant_dynamic-update-slice_fusion.1
  188.9 2.7 fusion.97
  191.6 3.1 convolution_convert_fusion.6
  196.4 4.5 %collective-permute-done.8 = bf16[256,1024]{1,0:T(8,128)(2,1)S(1)} collective-permute-done((bf16[256,1024]{1,0:T(8,128)(2,1)S(1)}, bf16[256,1024]{1,0:T(8,128)(2,1)S(1)}, u32[]{:S(2)}, u32[]{:S(2)}) %collective-permute-start.8) | collective-permute-done | bytes 524320 | tf_op jit(solution)/shard_map/ppermute | solution.py:138
  201.8 4.1 %multiply_convert_fusion = bf16[8,512,640]{2,1,0:T(8,128)(2,1)S(1)} fusion(f32[8,512,640]{2,1,0:T(8,128)S(1)} %bitcast.211, f32[8,512]{1,0:T(8,128)S(1)} %bitcast.253, f32[8,512]{1,0:T(8,128)S(1)} %log_add_fusion, pred[512,640]{1,0:T(8,128)(4,1)S(1)} %fusion.30, bf16[512,8,64]{0,2,1:T(8,128)(2,1)S(1)} %bitcast.251, bf16[640,8,64]{0,2,1:T(8,128)(2,1)S(1)} %bitcast.232), kind=kOutput, calls=%fused_computation | convolution fusion | flops 351272960 | bytes 17268736 | tf_op jit(solution)/shard_map/qhe,khe->hqk/dot_general | solution.py:263
  206.9 2.9 fusion.94
  211.6 7.8 %collective-permute-start.9 = (bf16[64,1024]{0,1:T(8,128)(2,1)S(1)}, bf16[64,1024]{0,1:T(8,128)(2,1)S(1)}, u32[]{:S(2)}, u32[]{:S(2)}) collective-permute-start(bf16[64,1024]{0,1:T(8,128)(2,1)S(1)} %get-tuple-element.186), channel_id=1, source_target_pairs={{0,2},{2,4},{4,6},{6,8},{8,10},{10,12},{12,14},{14,16},{16,18},{18... | collective-permute-start | bytes 393224 | tf_op jit(solution)/shard_map/ppermute | solution.py:167
  226.1 5.0 %scatter-add.6 = f32[512,1024]{0,1:T(8,128)S(1)} dynamic-update-slice(f32[512,1024]{0,1:T(8,128)S(1)} %fusion.15, f32[64,1024]{0,1:T(8,128)} %fusion.63, s32[]{:T(128)} %constant.199.clone.1, s32[]{:T(128)} %constant.199.clone.1) | dynamic-update-slice | bytes 524292 | tf_op jit(solution)/shard_map/scatter-add | solution.py:440
  232.3 4.4 %scatter-add.9 = f32[512,1024]{0,1:T(8,128)S(1)} dynamic-update-slice(f32[512,1024]{0,1:T(8,128)S(1)} %scatter-add.6, f32[64,1024]{0,1:T(8,128)} %slice_add_fusion, s32[]{:T(128)} %constant.217.clone.1, s32[]{:T(128)} %constant.199.clone.1) | dynamic-update-slice | bytes 524292 | tf_op jit(solution)/shard_map/scatter-add | solution.py:441
  242.8 3.1 convolution_convert_fusion.3
  248.6 58.7 %reduce-scatter.7.cloned.1.call-done = bf16[64,3936]{1,0:T(8,128)(2,1)} async-done(((bf16[1024,3936]{1,0:T(8,128)(2,1)}), bf16[64,3936]{1,0:T(8,128)(2,1)}) %reduce-scatter.7.cloned.1.call-update) | async-done | bytes 503824
  309.6 2.7 convert_element_type.186
  312.3 3.8 multiply_reduce_fusion.1
  328.1 4.5 %add_add_fusion = f32[256,1024]{1,0:T(8,128)} fusion(f32[256,1024]{1,0:T(8,128)S(1)} %copy-done.6, bf16[256,1024]{1,0:T(8,128)(2,1)} %collective-permute-done.5, bf16[1024,1312]{1,0:T(8,128)(2,1)} %all-gather.4.cloned.1.call-done, bf16[512,1312]{0,1:T(8,128)(2,1)} %copy-done.49, s32[]{:T(128)S(6)} %select_n.17), kind=kOutput, calls=%fused_computation.90 | convolution fusion | flops 688652288 | bytes 6176772 | tf_op jit(solution)/shard_map/dot_general | solution.py:297
  358.1 3.2 fusion.71
  370.6 14.2 %reduce-scatter.5.cloned.1.call-done = bf16[64,2048]{1,0:T(8,128)(2,1)} async-done(((bf16[1024,2048]{1,0:T(8,128)(2,1)}), bf16[64,2048]{1,0:T(8,128)(2,1)}) %reduce-scatter.5.cloned.1.call-update) | async-done | bytes 262160 | tf_op jit(solution)/shard_map/reduce_scatter | solution.py:459
  (266 shorter events, 110.4 us)
Async XLA Ops:
  7.2 135.9 %all-gather.6.cloned.1.call-start = ((), (), s32[]{:S(2)}) async-start(), calls=%async_computation.4 | async-start | bytes 3063808 | tf_op jit(solution)/shard_map/all_gather | solution.py:348
  9.2 138.9 %all-gather.4.cloned.1.call-start = ((), (), s32[]{:S(2)}) async-start(), calls=%async_computation.2 | async-start | bytes 3063808 | tf_op jit(solution)/shard_map/all_gather | solution.py:348
  12.0 72.1 %collective-permute-start = (bf16[256,1024]{1,0:T(8,128)(2,1)}, bf16[256,1024]{1,0:T(8,128)(2,1)}, u32[]{:S(2)}, u32[]{:S(2)}) collective-permute-start(bf16[256,1024]{1,0:T(8,128)(2,1)} %get-tuple-element.165), channel_id=1, source_target_pairs={{0,1},{1,0},{2,3},{3,2},{4,5},{5,4},{6,7},{7,6},{8,9},{9,8},{10,11... | collective-permute-start | bytes 1572872 | tf_op jit(solution)/shard_map/ppermute | solution.py:138
  15.7 291.5 %reduce-scatter.7.cloned.1.call-start = ((), (), s32[]{:S(2)}) async-start(), calls=%async_computation.5 | async-start | bytes 8634368
  81.9 58.1 %copy-start.2 = (bf16[1024,1312]{1,0:T(8,128)(2,1)}, bf16[1024,1312]{1,0:T(8,128)(2,1)S(1)}, u32[]{:S(2)}) copy-start(bf16[1024,1312]{1,0:T(8,128)(2,1)S(1)} %get-tuple-element.70) | copy-start | bytes 8060932
  90.9 5.3 %collective-permute-start.2 = (bf16[64,1024]{0,1:T(8,128)(2,1)S(1)}, bf16[64,1024]{0,1:T(8,128)(2,1)S(1)}, u32[]{:S(2)}, u32[]{:S(2)}) collective-permute-start(bf16[64,1024]{0,1:T(8,128)(2,1)S(1)} %get-tuple-element.199), channel_id=1, source_target_pairs={{2,0},{4,2},{6,4},{8,6},{10,8},{12,10},{14,12},{16,14},{18,16},{20... | collective-permute-start | bytes 393224 | tf_op jit(solution)/shard_map/ppermute | solution.py:168
  92.2 4.2 %collective-permute-start.1 = (bf16[64,1024]{0,1:T(8,128)(2,1)S(1)}, bf16[64,1024]{0,1:T(8,128)(2,1)S(1)}, u32[]{:S(2)}, u32[]{:S(2)}) collective-permute-start(bf16[64,1024]{0,1:T(8,128)(2,1)S(1)} %get-tuple-element.198), channel_id=1, source_target_pairs={{0,2},{2,4},{4,6},{6,8},{8,10},{10,12},{12,14},{14,16},{16,18},{18... | collective-permute-start | bytes 393224 | tf_op jit(solution)/shard_map/ppermute | solution.py:167
  107.5 10.0 %collective-permute-start.3 = (bf16[256,1024]{1,0:T(8,128)(2,1)S(1)}, bf16[256,1024]{1,0:T(8,128)(2,1)S(1)}, u32[]{:S(2)}, u32[]{:S(2)}) collective-permute-start(bf16[256,1024]{1,0:T(8,128)(2,1)S(1)} %convolution_convert_fusion.5), channel_id=1, source_target_pairs={{0,1},{1,0},{2,3},{3,2},{4,5},{5,4},{6,7},{7,6},{8,9},{9,8},{10,11... | collective-permute-start | bytes 1572872 | tf_op jit(solution)/shard_map/ppermute | solution.py:156
  110.1 18.6 %collective-permute-start.6 = (bf16[256,1024]{1,0:T(8,128)(2,1)S(1)}, bf16[256,1024]{1,0:T(8,128)(2,1)S(1)}, u32[]{:S(2)}, u32[]{:S(2)}) collective-permute-start(bf16[256,1024]{1,0:T(8,128)(2,1)S(1)} %get-tuple-element.161), channel_id=1, source_target_pairs={{0,1},{1,0},{2,3},{3,2},{4,5},{5,4},{6,7},{7,6},{8,9},{9,8},{10,11... | collective-permute-start | bytes 1572872 | tf_op jit(solution)/shard_map/ppermute | solution.py:138
  118.1 67.6 %copy-start.5 = (f32[256,1024]{1,0:T(8,128)}, f32[256,1024]{1,0:T(8,128)S(1)}, u32[]{:S(2)}) copy-start(f32[256,1024]{1,0:T(8,128)S(1)} %get-tuple-element.223) | copy-start | bytes 3145732
  118.7 21.2 %collective-permute-start.4 = (bf16[256,1024]{1,0:T(8,128)(2,1)S(1)}, bf16[256,1024]{1,0:T(8,128)(2,1)S(1)}, u32[]{:S(2)}, u32[]{:S(2)}) collective-permute-start(bf16[256,1024]{1,0:T(8,128)(2,1)S(1)} %get-tuple-element.163), channel_id=1, source_target_pairs={{0,1},{1,0},{2,3},{3,2},{4,5},{5,4},{6,7},{7,6},{8,9},{9,8},{10,11... | collective-permute-start | bytes 1572872 | tf_op jit(solution)/shard_map/ppermute | solution.py:138
  161.9 11.1 %collective-permute-start.7 = (bf16[256,1024]{1,0:T(8,128)(2,1)S(1)}, bf16[256,1024]{1,0:T(8,128)(2,1)S(1)}, u32[]{:S(2)}, u32[]{:S(2)}) collective-permute-start(bf16[256,1024]{1,0:T(8,128)(2,1)S(1)} %fusion.31), channel_id=1, source_target_pairs={{0,1},{1,0},{2,3},{3,2},{4,5},{5,4},{6,7},{7,6},{8,9},{9,8},{10,11... | collective-permute-start | bytes 1572872 | tf_op jit(solution)/shard_map/ppermute | solution.py:394
  185.0 199.8 %reduce-scatter.5.cloned.1.call-start = ((), (), s32[]{:S(2)}) async-start(), calls=%async_computation.3 | async-start | bytes 4456448 | tf_op jit(solution)/shard_map/reduce_scatter | solution.py:459
  185.1 16.6 %slice-start = ((s8[10485760]{0:T(1024)(128)(4,1)}), s8[4194304]{0:T(1024)(128)(4,1)S(1)}, s32[]{:S(2)}) async-start(s8[10485760]{0:T(1024)(128)(4,1)} %bitcast.210), calls=%async_computation.6 | async-start | bytes 8388608
  185.7 16.0 %slice-start.1 = ((s8[10485760]{0:T(1024)(128)(4,1)}), s8[4194304]{0:T(1024)(128)(4,1)S(1)}, s32[]{:S(2)}) async-start(s8[10485760]{0:T(1024)(128)(4,1)} %bitcast.210), calls=%async_computation.7 | async-start | bytes 8388608
  188.6 12.2 %collective-permute-start.8 = (bf16[256,1024]{1,0:T(8,128)(2,1)S(1)}, bf16[256,1024]{1,0:T(8,128)(2,1)S(1)}, u32[]{:S(2)}, u32[]{:S(2)}) collective-permute-start(bf16[256,1024]{1,0:T(8,128)(2,1)S(1)} %get-tuple-element.158), channel_id=1, source_target_pairs={{0,1},{1,0},{2,3},{3,2},{4,5},{5,4},{6,7},{7,6},{8,9},{9,8},{10,11... | collective-permute-start | bytes 1572872 | tf_op jit(solution)/shard_map/ppermute | solution.py:138
  194.7 133.3 %collective-permute-start.5 = (bf16[256,1024]{1,0:T(8,128)(2,1)}, bf16[256,1024]{1,0:T(8,128)(2,1)}, u32[]{:S(2)}, u32[]{:S(2)}) collective-permute-start(bf16[256,1024]{1,0:T(8,128)(2,1)} %convolution_convert_fusion.6), channel_id=1, source_target_pairs={{0,1},{1,0},{2,3},{3,2},{4,5},{5,4},{6,7},{7,6},{8,9},{9,8},{10,11... | collective-permute-start | bytes 1572872 | tf_op jit(solution)/shard_map/ppermute | solution.py:156
  210.2 14.6 %collective-permute-start.10 = (bf16[64,1024]{0,1:T(8,128)(2,1)S(1)}, bf16[64,1024]{0,1:T(8,128)(2,1)S(1)}, u32[]{:S(2)}, u32[]{:S(2)}) collective-permute-start(bf16[64,1024]{0,1:T(8,128)(2,1)S(1)} %get-tuple-element.187), channel_id=1, source_target_pairs={{2,0},{4,2},{6,4},{8,6},{10,8},{12,10},{14,12},{16,14},{18,16},{20... | collective-permute-start | bytes 393224 | tf_op jit(solution)/shard_map/ppermute | solution.py:168
  211.6 13.2 %collective-permute-start.9 = (bf16[64,1024]{0,1:T(8,128)(2,1)S(1)}, bf16[64,1024]{0,1:T(8,128)(2,1)S(1)}, u32[]{:S(2)}, u32[]{:S(2)}) collective-permute-start(bf16[64,1024]{0,1:T(8,128)(2,1)S(1)} %get-tuple-element.186), channel_id=1, source_target_pairs={{0,2},{2,4},{4,6},{6,8},{8,10},{10,12},{12,14},{14,16},{16,18},{18... | collective-permute-start | bytes 393224 | tf_op jit(solution)/shard_map/ppermute | solution.py:167
  242.4 70.0 %collective-permute-start.11 = (bf16[256,1024]{1,0:T(8,128)(2,1)}, bf16[256,1024]{1,0:T(8,128)(2,1)}, u32[]{:S(2)}, u32[]{:S(2)}) collective-permute-start(bf16[256,1024]{1,0:T(8,128)(2,1)} %convolution_convert_fusion.7), channel_id=1, source_target_pairs={{0,1},{1,0},{2,3},{3,2},{4,5},{5,4},{6,7},{7,6},{8,9},{9,8},{10,11... | collective-permute-start | bytes 1572872 | tf_op jit(solution)/shard_map/ppermute | solution.py:156
  316.2 11.7 %collective-permute-start.12 = (f32[2,1024]{1,0:T(2,128)S(1)}, f32[2,1024]{1,0:T(2,128)S(1)}, u32[]{:S(2)}, u32[]{:S(2)}) collective-permute-start(f32[2,1024]{1,0:T(2,128)S(1)} %pad_maximum_fusion.16), channel_id=1, source_target_pairs={{0,1},{1,0},{2,3},{3,2},{4,5},{5,4},{6,7},{7,6},{8,9},{9,8},{10,11... | collective-permute-start | bytes 24584 | tf_op jit(solution)/shard_map/ppermute | solution.py:127
  327.9 14.1 %copy-start.8 = (f32[256,1024]{1,0:T(8,128)S(1)}, f32[256,1024]{1,0:T(8,128)}, u32[]{:S(2)}) copy-start(f32[256,1024]{1,0:T(8,128)} %param.21) | copy-start | bytes 3145732
  327.9 14.0 %copy-start.17 = (f32[256,1024]{1,0:T(8,128)S(1)}, f32[256,1024]{1,0:T(8,128)}, u32[]{:S(2)}) copy-start(f32[256,1024]{1,0:T(8,128)} %get-tuple-element.159) | copy-start | bytes 3145732
  327.9 14.0 %copy-start.36 = (f32[256,1024]{1,0:T(8,128)S(1)}, f32[256,1024]{1,0:T(8,128)}, u32[]{:S(2)}) copy-start(f32[256,1024]{1,0:T(8,128)} %get-tuple-element.228) | copy-start | bytes 3145732
  328.0 4.6 %collective-permute-start.13 = (f32[2,1024]{1,0:T(2,128)S(1)}, f32[2,1024]{1,0:T(2,128)S(1)}, u32[]{:S(2)}, u32[]{:S(2)}) collective-permute-start(f32[2,1024]{1,0:T(2,128)S(1)} %fusion.93), channel_id=1, source_target_pairs={{0,2},{2,0},{4,6},{6,4},{8,10},{10,8},{12,14},{14,12},{16,18},{18,... | collective-permute-start | bytes 24584 | tf_op jit(solution)/shard_map/ppermute | solution.py:127
  332.6 3.7 collective-permute-start.14
  336.3 3.7 collective-permute-start.15
  340.0 4.7 %collective-permute-start.16 = (f32[2,1024]{1,0:T(2,128)S(1)}, f32[2,1024]{1,0:T(2,128)S(1)}, u32[]{:S(2)}, u32[]{:S(2)}) collective-permute-start(f32[2,1024]{1,0:T(2,128)S(1)} %add.291), channel_id=1, source_target_pairs={{0,16},{2,18},{4,20},{6,22},{8,24},{10,26},{12,28},{14,30},{16,0},... | collective-permute-start | bytes 24584 | tf_op jit(solution)/shard_map/ppermute | solution.py:127
  368.1 16.8 %copy-start.26 = (f32[2,64,1536]{2,1,0:T(8,128)S(1)}, f32[2,64,1536]{2,1,0:T(8,128)}, u32[]{:S(2)}) copy-start(f32[2,64,1536]{2,1,0:T(8,128)} %param.29) | copy-start | bytes 2359300
  368.1 17.9 %copy-start.30 = (f32[64,1536]{1,0:T(8,128)S(1)}, f32[64,1536]{1,0:T(8,128)}, u32[]{:S(2)}) copy-start(f32[64,1536]{1,0:T(8,128)} %param.24) | copy-start | bytes 1179652
  370.6 16.4 %copy-start.41 = (f32[2,512,64]{1,2,0:T(8,128)S(1)}, f32[2,512,64]{1,2,0:T(8,128)}, u32[]{:S(2)}) copy-start(f32[2,512,64]{1,2,0:T(8,128)} %param.30) | copy-start | bytes 786436
  370.6 16.5 %copy-start.46 = (f32[512,64]{0,1:T(8,128)S(1)}, f32[512,64]{0,1:T(8,128)}, u32[]{:S(2)}) copy-start(f32[512,64]{0,1:T(8,128)} %param.25) | copy-start | bytes 393220
  (46 other events, 242.3 us)
Sparse Core Ops, SparseCore 0:
  10.9 63.2 all-gather.5
  77.0 45.3 all-gather.3
  185.1 122.0 reduce-scatter.6
  312.4 72.3 reduce-scatter.4
